TPU v7x, 32 devices: a whole 2x2x4 slice. The times are simulated.
32 devices in a mesh: group: 2 (over x), blk: 16 (over z, y, core).
Axes of the slice: x: 2, y: 2, z: 4, core: 2. Of those that a mesh axis runs over, the one named last changes fastest.
Arguments:
- tensors: bfloat16 [64, 256, 4, 256], P(('group', 'blk')), parts along dimension 0, may hold values from -6 to 6
- gate_terms: float32 [2, 16, 16], replicated, may hold values from -1.2 to 1.2
- right_proj: bfloat16 [32, 1024, 256], P('blk')
- left_proj: bfloat16 [32, 256, 1024], P('blk'), may hold values from -0.1875 to 0.1875
Outputs:
- evolved: bfloat16 [64, 256, 4, 256], P(('group', 'blk')), parts along dimension 0
- records: float32 [8, 2], P('group'), parts along dimension 0
There are 2 independent parts, one for each index of `group`. A program takes and returns all parts, laid end to end along the dimension named above; an argument that names none is the same for every part. Nothing has to cross between parts.
All inputs are finite; a program needn't handle non-finite values.
Results may differ from a plain program's by a relative error of at most 0.024.
Values may be sent and summed in bfloat16 or wider, within the bound.
A program may use at most 64 MiB of HBM per device.

v0:
```python
import functools
import jax
import jax.numpy as jnp
from jax import lax
from jax.experimental import pallas as pl
from jax.experimental.pallas import tpu as pltpu
from jax.sharding import PartitionSpec as P

LAYERS = 4
HALF = 128
GROUP = 16


def mm(a, b):
    return jnp.dot(a, b, preferred_element_type=jnp.float32)


def sweep_kernel(n, chi, d, entries, x_ref, w_ref, rp_ref, lp_ref, out_ref, rec_ref,
                 site_a, site_b, ahead, back, r_in, a_in, gated, lp_perm, acc, mine, seen,
                 fs, fr, bs, br, ss, sr):
    me = lax.axis_index("blk")
    right, left = lax.rem(me + 1, n), lax.rem(me + n - 1, n)
    quarter = chi // d
    barrier = pltpu.get_barrier_semaphore()

    def greet(k, carry):
        pl.semaphore_signal(barrier, inc=1, device_id={"blk": lax.rem(me + k, n)},
                            device_id_type=pl.DeviceIdType.MESH)
        return carry

    lax.fori_loop(1, n, greet, 0)

    rows = lax.broadcasted_iota(jnp.int32, (chi, chi), 0)
    cols = lax.broadcasted_iota(jnp.int32, (chi, chi), 1)
    to_block = jnp.where((rows // quarter == cols % d) & (rows % quarter == cols // d), 1.0, 0.0).astype(jnp.bfloat16)
    to_plain = jnp.where((cols // quarter == rows % d) & (cols % quarter == rows // d), 1.0, 0.0).astype(jnp.bfloat16)
    wide = d * HALF
    wrow = lax.broadcasted_iota(jnp.int32, (wide, wide), 0)
    wcol = lax.broadcasted_iota(jnp.int32, (wide, wide), 1)
    spread = jnp.where((wcol // HALF == wrow % d) & (wcol % HALF == wrow // d), 1.0, 0.0).astype(jnp.bfloat16)

    for which, site in ((0, site_a), (1, site_b)):
        def load(k, carry, which=which, site=site):
            block = mm(to_block, x_ref[which, pl.ds(k * chi, chi), :]).astype(jnp.bfloat16)
            for p in range(d):
                for h in range(2):
                    site[h, pl.ds(p * chi + k * quarter, quarter), :] = block[p * quarter:(p + 1) * quarter, h * HALF:(h + 1) * HALF]
            return carry
        lax.fori_loop(0, d, load, 0)
    for parity in range(2):
        for k in range(2):
            part = mm(lp_ref[parity, :, k * wide:(k + 1) * wide], spread).astype(jnp.bfloat16)
            for s in range(d):
                lp_perm[parity, :, s * chi + k * HALF:s * chi + (k + 1) * HALF] = part[:, s * HALF:(s + 1) * HALF]

    def theta_gate(h, parity, lhs_ref, rhs_ref):
        def tile(at, carry):
            lhs = jnp.concatenate([
                jnp.concatenate([lhs_ref[q, pl.ds(u * chi + at * quarter, quarter), :] for q in range(2)], axis=1)
                for u in range(d)], axis=0)
            rhs = jnp.concatenate([rhs_ref[h, v * chi:(v + 1) * chi, :] for v in range(d)], axis=1)
            th = mm(lhs, rhs).astype(jnp.bfloat16)
            for pair in range(quarter // GROUP // 2):
                stack = jnp.concatenate([
                    jnp.concatenate([
                        th[u * quarter + (2 * pair + j) * GROUP:u * quarter + (2 * pair + j + 1) * GROUP, v * HALF:(v + 1) * HALF]
                        for v in range(d) for u in range(d)], axis=0)
                    for j in range(2)], axis=1)
                mixed = mm(w_ref[parity], stack)
                mixed = (mixed[:chi] + mixed[chi:]).astype(jnp.bfloat16)
                for j in range(2):
                    for t in range(d):
                        for s in range(d):
                            top = (t * d + s) * GROUP
                            gated[h, pl.ds(s * chi + at * quarter + (2 * pair + j) * GROUP, GROUP), t * HALF:(t + 1) * HALF] = (
                                mixed[top:top + GROUP, j * HALF:(j + 1) * HALF])
            return carry
        lax.fori_loop(0, d, tile, 0)

    def note(value):
        folded = value.reshape(value.shape[0] // 8, 8, value.shape[1])
        sq = jnp.sum(folded * folded, axis=0)
        mx = jnp.max(jnp.abs(folded), axis=0)
        for c in range(value.shape[1] // HALF):
            acc[0] += sq[:, c * HALF:(c + 1) * HALF]
            acc[1] = jnp.maximum(acc[1], mx[:, c * HALF:(c + 1) * HALF])

    def new_right(h, parity, dst, scale):
        value = mm(lp_perm[parity], gated[h])
        if scale is not None:
            value = value * scale
        note(value)
        value = value.astype(jnp.bfloat16)
        for t in range(d):
            dst[h, t * chi:(t + 1) * chi, :] = value[:, t * HALF:(t + 1) * HALF]

    def new_left(parity, dst, scale):
        def tile(s, carry):
            here = pl.ds(s * chi, chi)
            lhs = jnp.concatenate([gated[0, here, :], gated[1, here, :]], axis=1)
            rhs = jnp.concatenate([rp_ref[parity, t * chi + h * HALF:t * chi + (h + 1) * HALF, :]
                                   for h in range(2) for t in range(d)], axis=0)
            value = mm(lhs, rhs)
            if scale is not None:
                value = value * scale
            note(value)
            value = value.astype(jnp.bfloat16)
            for h in range(2):
                dst[h, here, :] = value[:, h * HALF:(h + 1) * HALF]
            return carry
        lax.fori_loop(0, d, tile, 0)

    def forward(k, h):
        return pltpu.make_async_remote_copy(
            src_ref=ahead.at[k, h], dst_ref=r_in.at[k, h], send_sem=fs.at[k, h], recv_sem=fr.at[k, h],
            device_id={"blk": left}, device_id_type=pl.DeviceIdType.MESH)

    def backward(k, h):
        return pltpu.make_async_remote_copy(
            src_ref=back.at[k, h], dst_ref=a_in.at[k, h], send_sem=bs.at[k, h], recv_sem=br.at[k, h],
            device_id={"blk": right}, device_id_type=pl.DeviceIdType.MESH)

    def everyone(layer):
        return pltpu.make_async_remote_copy(
            src_ref=seen.at[layer], dst_ref=seen.at[layer], send_sem=ss.at[layer], recv_sem=sr.at[layer],
            device_id={"blk": right}, device_id_type=pl.DeviceIdType.MESH)

    def share(layer):
        mine[layer, 0:1, :] = jnp.sum(acc[0], axis=0, keepdims=True)
        mine[layer, 1:2, :] = jnp.max(acc[1], axis=0, keepdims=True)

        def send(k, carry):
            pltpu.make_async_remote_copy(
                src_ref=mine.at[layer], dst_ref=seen.at[layer, k - 1], send_sem=ss.at[layer], recv_sem=sr.at[layer],
                device_id={"blk": lax.rem(me + k, n)}, device_id_type=pl.DeviceIdType.MESH).start()
            return carry
        lax.fori_loop(1, n, send, 0)
        acc[...] = jnp.zeros_like(acc)

    def learn(layer):
        everyone(layer).wait_recv()
        got = seen[layer]
        own = mine[layer]
        squares = jnp.sum(jnp.sum(got, axis=0)[0:1] + own[0:1], axis=1, keepdims=True)
        largest = jnp.max(jnp.maximum(jnp.max(got, axis=0)[1:2], own[1:2]), axis=1, keepdims=True)
        power = squares / entries + 1e-06
        root = jnp.sqrt(power)
        lane = lax.broadcasted_iota(jnp.int32, (1, HALF), 1)
        rec_ref[layer:layer + 1, :] = jnp.where(lane == 0, jnp.log(root), jnp.log(largest / root))
        return power, root

    acc[...] = jnp.zeros_like(acc)
    scale, root = None, None
    for layer in range(LAYERS):
        parity, k = layer % 2, layer // 2
        if parity == 0:
            lhs = site_a
            if k > 0:
                lhs = a_in.at[k - 1]
                for h in range(2):
                    backward(k - 1, h).wait_recv()
            for h in range(2):
                theta_gate(h, parity, lhs, site_b)
            if layer > 0:
                power, root = learn(layer - 1)
                scale = 1.0 / power
            new_left(parity, ahead.at[k], scale)
            if layer == 0:
                pl.semaphore_wait(barrier, n - 1)
            for h in range(2):
                forward(k, h).start()
            for h in range(2):
                new_right(h, parity, site_b, scale)
        else:
            for h in range(2):
                forward(k, h).wait_recv()
                theta_gate(h, parity, site_b, r_in.at[k])
                if h == 0:
                    power, root = learn(layer - 1)
                    scale = 1.0 / power
                new_right(h, parity, back.at[k], scale)
                backward(k, h).start()
            new_left(parity, site_b, scale)
        share(layer)

    last = LAYERS // 2 - 1
    for h in range(2):
        backward(last, h).wait_recv()
    power, root = learn(LAYERS - 1)
    shrink = 1.0 / root
    for which, site in ((0, a_in.at[last]), (1, site_b)):
        def store(kk, carry, which=which, site=site):
            block = jnp.concatenate([
                jnp.concatenate([site[h, pl.ds(p * chi + kk * quarter, quarter), :] for h in range(2)], axis=1)
                for p in range(d)], axis=0)
            out_ref[which, pl.ds(kk * chi, chi), :] = (mm(to_plain, block) * shrink).astype(jnp.bfloat16)
            return carry
        lax.fori_loop(0, d, store, 0)
    for k in range(LAYERS // 2):
        for h in range(2):
            forward(k, h).wait_send()
            backward(k, h).wait_send()
    for layer in range(LAYERS):
        everyone(layer).wait_send()


def local(tensors, gate_terms, right_proj, left_proj):
    slots, chi, d, _ = tensors.shape
    n = lax.axis_size("blk")
    entries = float(n * slots * chi * d * chi)
    table = jnp.eye(d * d, dtype=jnp.float32)[None] + gate_terms
    table = table.reshape(2, d, d, d, d).transpose(0, 2, 1, 4, 3).reshape(2, d * d, d * d)
    high = lax.reduce_precision(table, 8, 7)
    both = jnp.concatenate([high, table - high], axis=1)
    eye = jnp.eye(GROUP, dtype=jnp.float32)
    mixer = (both[:, :, None, :, None] * eye[None, None, :, None, :]).reshape(2, 2 * d * d * GROUP, d * d * GROUP)
    mixer = mixer.astype(jnp.bfloat16)
    vmem = pl.BlockSpec(memory_space=pltpu.VMEM)
    half = (2, d * chi, HALF)
    dma = pltpu.SemaphoreType.DMA
    pairs = LAYERS // 2
    evolved, records = pl.pallas_call(
        functools.partial(sweep_kernel, n, chi, d, entries),
        out_shape=(jax.ShapeDtypeStruct((2, chi * d, chi), jnp.bfloat16),
                   jax.ShapeDtypeStruct((8, HALF), jnp.float32)),
        in_specs=[vmem] * 4,
        out_specs=(vmem, vmem),
        scratch_shapes=[
            pltpu.VMEM(half, jnp.bfloat16),
            pltpu.VMEM(half, jnp.bfloat16),
            pltpu.VMEM((pairs,) + half, jnp.bfloat16),
            pltpu.VMEM((pairs,) + half, jnp.bfloat16),
            pltpu.VMEM((pairs,) + half, jnp.bfloat16),
            pltpu.VMEM((pairs,) + half, jnp.bfloat16),
            pltpu.VMEM((2, d * chi, d * HALF), jnp.bfloat16),
            pltpu.VMEM((2, chi, d * chi), jnp.bfloat16),
            pltpu.VMEM((2, 8, HALF), jnp.float32),
            pltpu.VMEM((LAYERS, 2, HALF), jnp.float32),
            pltpu.VMEM((LAYERS, n - 1, 2, HALF), jnp.float32),
            dma((pairs, 2)), dma((pairs, 2)), dma((pairs, 2)), dma((pairs, 2)),
            dma((LAYERS,)), dma((LAYERS,)),
        ],
        compiler_params=pltpu.CompilerParams(collective_id=0, has_side_effects=True,
                                             vmem_limit_bytes=56 * 1024 * 1024),
        name="sweep",
    )(tensors.reshape(slots, chi * d, chi), mixer, right_proj, left_proj)
    return evolved.reshape(tensors.shape), records[:LAYERS, :2]


def solution(mesh):
    in_specs = (
        P(("group", "blk"), None, None, None),
        P(),
        P("blk", None, None),
        P("blk", None, None),
    )
    out_specs = (P(("group", "blk"), None, None, None), P("group", None))
    return jax.shard_map(local, mesh=mesh, in_specs=in_specs, out_specs=out_specs, check_vma=False)
```

profile of v0, /device:TPU:3, one launch (start us, length us, event | category | flops | bytes accessed | tf_op | source)
XLA Modules:
  0.0 80.8 jit_solution(4633687084060836392)
XLA Ops:
  0.6 0.7 broadcast_add_fusion
  1.4 0.1 reshape.37
  1.5 0.3 copy.7
  1.8 0.1 reshape.38
  1.9 3.8 %mul.20 = f32[2,32,16,16,16]{4,3,2,1,0:T(8,128)} broadcast(f32[2,32,16]{2,1,0:T(8,128)S(1)} %pad_maximum_fusion), dimensions={0,1,3} | broadcast | bytes 1052672 | tf_op jit(solution)/shard_map/mul | solution.py:216
  5.7 0.0 copy-start
  5.7 6.2 %mul.21 = f32[2,512,256]{2,1,0:T(8,128)S(1)} reshape(f32[2,32,16,16,16]{4,3,2,1,0:T(8,128)} %mul.20) | data formatting | bytes 2097152 | tf_op jit(solution)/shard_map/mul | solution.py:216
  11.9 2.4 %mul.22 = f32[32,16,16,16]{3,2,1,0:T(8,128)} broadcast(f32[16,16]{1,0:T(8,128)S(1)} %fusion), dimensions={1,3} | broadcast | bytes 525312 | tf_op jit(solution)/shard_map/mul | solution.py:216
  14.3 3.5 %mul.23 = f32[512,256]{1,0:T(8,128)S(1)} reshape(f32[32,16,16,16]{3,2,1,0:T(8,128)} %mul.22) | data formatting | bytes 1048576 | tf_op jit(solution)/shard_map/mul | solution.py:216
  17.8 0.9 %multiply_convert_fusion.w_ref = bf16[2,512,256]{2,1,0:T(8,128)(2,1)} fusion(f32[2,512,256]{2,1,0:T(8,128)S(1)} %mul.21, f32[512,256]{1,0:T(8,128)S(1)} %mul.23), kind=kLoop, calls=%fused_computation | loop fusion | flops 524288 | bytes 2097152 | tf_op jit(solution)/shard_map/convert_element_type | solution.py:217
  18.7 0.0 copy-done
  18.7 1.1 %reshape.36.x_ref = bf16[2,1024,256]{2,1,0:T(8,128)(2,1)} reshape(bf16[2,256,4,256]{3,2,1,0:T(4,128)(2,1)S(1)} %copy-done) | data formatting | bytes 2097152 | tf_op jit(solution)/shard_map/reshape | solution.py:246
  19.8 57.5 %sweep.1 = (bf16[2,1024,256]{2,1,0:T(8,128)(2,1)}, f32[8,128]{1,0:T(8,128)}) custom-call(bf16[2,1024,256]{2,1,0:T(8,128)(2,1)} %reshape.36.x_ref, bf16[2,512,256]{2,1,0:T(8,128)(2,1)} %multiply_convert_fusion.w_ref, bf16[2,1024,256]{2,1,0:T(8,128)(2,1)} %rp_ref.1, bf16[2,256,1024]{2,1,0:T(8,128)(2,1)} %lp_ref.1), custom_call_target="tpu_custom_call" | custom-call | tf_op jit(solution)/shard_map/sweep/pallas_call | solution.py:222
  77.4 2.1 %reshape.39 = bf16[2,256,4,256]{3,2,1,0:T(4,128)(2,1)} reshape(bf16[2,1024,256]{2,1,0:T(8,128)(2,1)} %get-tuple-element.4) | data formatting | bytes 2097152 | tf_op jit(solution)/shard_map/reshape | solution.py:247
  79.5 0.7 slice.3
  80.2 0.7 copy.8
  (3 shorter events, 0.0 us)
Async XLA Ops:
  5.7 13.0 %copy-start = (bf16[2,256,4,256]{3,2,1,0:T(4,128)(2,1)S(1)}, bf16[2,256,4,256]{3,2,1,0:T(4,128)(2,1)}, u32[]{:S(2)}) copy-start(bf16[2,256,4,256]{3,2,1,0:T(4,128)(2,1)} %param.4) | copy-start | bytes 3145732
where the time goes:
time: 81.2 us; the launch traced here: 80.8 us
  Pallas kernels  57.5 us (71%)
  local copies, waits for them, and re-layouts  21 us (26%)
  other arithmetic  1.66 us (2%)
    pallas_call x1, Pallas kernels, local(): pl.pallas_call(functools.partial(sweep_kernel, n, chi, d, entries), out_s...  57.5 us
    mul x4, local copies, waits for them, and re-layouts, local(): both[:, :, None, :, None] * eye[None, None, :, None, :]  15.9 us
    reshape x1, local copies, waits for them, and re-layouts, local(): return (evolved.reshape(tensors.shape), records[:LAYERS, :2])  2.14 us

commit v1 on v0

--- a/solution.py
+++ b/solution.py
@@ -15,8 +15,8 @@
     return jnp.dot(a, b, preferred_element_type=jnp.float32)
 
 
-def sweep_kernel(n, chi, d, entries, x_ref, w_ref, rp_ref, lp_ref, out_ref, rec_ref,
-                 site_a, site_b, ahead, back, r_in, a_in, gated, lp_perm, acc, mine, seen,
+def sweep_kernel(n, chi, d, entries, x_ref, gate_ref, rp_ref, lp_ref, out_ref, rec_ref,
+                 w_ref, site_a, site_b, ahead, back, r_in, a_in, gated, lp_perm, acc, mine, seen,
                  fs, fr, bs, br, ss, sr):
     me = lax.axis_index("blk")
     right, left = lax.rem(me + 1, n), lax.rem(me + n - 1, n)
@@ -39,9 +39,32 @@
     wcol = lax.broadcasted_iota(jnp.int32, (wide, wide), 1)
     spread = jnp.where((wcol // HALF == wrow % d) & (wcol % HALF == wrow // d), 1.0, 0.0).astype(jnp.bfloat16)
 
+    pairs = d * d
+    pick_row = lax.broadcasted_iota(jnp.int32, (chi, pairs), 0) // GROUP
+    pick_from = lax.broadcasted_iota(jnp.int32, (chi, pairs), 1)
+    pick_left = jnp.where(pick_from == (pick_row % d) * d + pick_row // d, 1.0, 0.0).astype(jnp.bfloat16)
+    pick_col = lax.broadcasted_iota(jnp.int32, (pairs, chi), 1) // GROUP
+    pick_into = lax.broadcasted_iota(jnp.int32, (pairs, chi), 0)
+    pick_right = jnp.where(pick_into == (pick_col % d) * d + pick_col // d, 1.0, 0.0).astype(jnp.bfloat16)
+    same = rows % GROUP == cols % GROUP
+    unit = jnp.where(lax.broadcasted_iota(jnp.int32, (pairs, pairs), 0)
+                     == lax.broadcasted_iota(jnp.int32, (pairs, pairs), 1), 1.0, 0.0)
+
+    def mixer(parity):
+        table = unit + gate_ref[parity]
+        high = table.astype(jnp.bfloat16)
+        low = (table - high.astype(jnp.float32)).astype(jnp.bfloat16)
+        for position, term in ((0, high), (1, low)):
+            spread_rows = mm(pick_left, term).astype(jnp.bfloat16)
+            full = jnp.where(same, mm(spread_rows, pick_right), 0.0)
+            w_ref[parity, position * chi:(position + 1) * chi, :] = full.astype(jnp.bfloat16)
+
+    mixer(0)
+    mixer(1)
+
     for which, site in ((0, site_a), (1, site_b)):
         def load(k, carry, which=which, site=site):
-            block = mm(to_block, x_ref[which, pl.ds(k * chi, chi), :]).astype(jnp.bfloat16)
+            block = mm(to_block, x_ref[which, pl.ds(k * quarter, quarter)].reshape(chi, chi)).astype(jnp.bfloat16)
             for p in range(d):
                 for h in range(2):
                     site[h, pl.ds(p * chi + k * quarter, quarter), :] = block[p * quarter:(p + 1) * quarter, h * HALF:(h + 1) * HALF]
@@ -145,7 +168,7 @@
         largest = jnp.max(jnp.maximum(jnp.max(got, axis=0)[1:2], own[1:2]), axis=1, keepdims=True)
         power = squares / entries + 1e-06
         root = jnp.sqrt(power)
-        lane = lax.broadcasted_iota(jnp.int32, (1, HALF), 1)
+        lane = lax.broadcasted_iota(jnp.int32, (1, 2), 1)
         rec_ref[layer:layer + 1, :] = jnp.where(lane == 0, jnp.log(root), jnp.log(largest / root))
         return power, root
 
@@ -193,7 +216,7 @@
             block = jnp.concatenate([
                 jnp.concatenate([site[h, pl.ds(p * chi + kk * quarter, quarter), :] for h in range(2)], axis=1)
                 for p in range(d)], axis=0)
-            out_ref[which, pl.ds(kk * chi, chi), :] = (mm(to_plain, block) * shrink).astype(jnp.bfloat16)
+            out_ref[which, pl.ds(kk * quarter, quarter)] = (mm(to_plain, block) * shrink).astype(jnp.bfloat16).reshape(quarter, d, chi)
             return carry
         lax.fori_loop(0, d, store, 0)
     for k in range(LAYERS // 2):
@@ -208,24 +231,18 @@
     slots, chi, d, _ = tensors.shape
     n = lax.axis_size("blk")
     entries = float(n * slots * chi * d * chi)
-    table = jnp.eye(d * d, dtype=jnp.float32)[None] + gate_terms
-    table = table.reshape(2, d, d, d, d).transpose(0, 2, 1, 4, 3).reshape(2, d * d, d * d)
-    high = lax.reduce_precision(table, 8, 7)
-    both = jnp.concatenate([high, table - high], axis=1)
-    eye = jnp.eye(GROUP, dtype=jnp.float32)
-    mixer = (both[:, :, None, :, None] * eye[None, None, :, None, :]).reshape(2, 2 * d * d * GROUP, d * d * GROUP)
-    mixer = mixer.astype(jnp.bfloat16)
     vmem = pl.BlockSpec(memory_space=pltpu.VMEM)
     half = (2, d * chi, HALF)
     dma = pltpu.SemaphoreType.DMA
     pairs = LAYERS // 2
     evolved, records = pl.pallas_call(
         functools.partial(sweep_kernel, n, chi, d, entries),
-        out_shape=(jax.ShapeDtypeStruct((2, chi * d, chi), jnp.bfloat16),
-                   jax.ShapeDtypeStruct((8, HALF), jnp.float32)),
+        out_shape=(jax.ShapeDtypeStruct(tensors.shape, jnp.bfloat16),
+                   jax.ShapeDtypeStruct((LAYERS, 2), jnp.float32)),
         in_specs=[vmem] * 4,
         out_specs=(vmem, vmem),
         scratch_shapes=[
+            pltpu.VMEM((2, 2 * d * d * GROUP, d * d * GROUP), jnp.bfloat16),
             pltpu.VMEM(half, jnp.bfloat16),
             pltpu.VMEM(half, jnp.bfloat16),
             pltpu.VMEM((pairs,) + half, jnp.bfloat16),
@@ -243,8 +260,8 @@
         compiler_params=pltpu.CompilerParams(collective_id=0, has_side_effects=True,
                                              vmem_limit_bytes=56 * 1024 * 1024),
         name="sweep",
-    )(tensors.reshape(slots, chi * d, chi), mixer, right_proj, left_proj)
-    return evolved.reshape(tensors.shape), records[:LAYERS, :2]
+    )(tensors, gate_terms, right_proj, left_proj)
+    return evolved, records
 
 
 def solution(mesh):

time: 81.2 us -> 62.6 us (0.77)
  local copies, waits for them, and re-layouts: 21 us -> 3.85 us
  other arithmetic: 1.66 us -> 0 us
    mul x4 -> x0, local copies, waits for them, and re-layouts: 15.9 us -> none  [local(): both[:, :, None, :, None] * eye[None, None, :, None, :]]
    reshape x5 -> x0, local copies, waits for them, and re-layouts: 3.72 us -> none  [the longest x1 2.14 us: local(): return (evolved.reshape(tensors.shape), records[:LAYERS, :2])]
    unnamed x3, local copies, waits for them, and re-layouts: 0.65 us -> 3.2 us
    convert_element_type x2 -> x0, other arithmetic: 0.92 us -> none  [the longest x1 0.91 us: local(): mixer = mixer.astype(jnp.bfloat16)]
where the time goes in v1:
time: 62.6 us; the launch traced here: 62.4 us
  Pallas kernels  57.9 us (92%)
  local copies, waits for them, and re-layouts  3.85 us (6%)
  between operations  0.65 us (1%)
    pallas_call x1, Pallas kernels, local(): pl.pallas_call(functools.partial(sweep_kernel, n, chi, d, entries), out_s...  57.9 us
    unnamed x3, local copies, waits for them, and re-layouts  3.2 us

profile of v1, /device:TPU:3, one launch (start us, length us, event | category | flops | bytes accessed | tf_op | source)
XLA Modules:
  0.0 62.4 jit_solution(12282330498834327991)
XLA Ops:
  0.6 57.9 %sweep.1 = (bf16[2,256,4,256]{3,2,1,0:T(4,128)(2,1)}, f32[4,2]{1,0:T(4,128)}) custom-call(bf16[2,256,4,256]{3,2,1,0:T(4,128)(2,1)} %x_ref.1, f32[2,16,16]{2,1,0:T(8,128)} %gate_ref.1, bf16[2,1024,256]{2,1,0:T(8,128)(2,1)} %rp_ref.1, bf16[2,256,1024]{2,1,0:T(8,128)(2,1)} %lp_ref.1), custom_call_target="tpu_custom_call" | custom-call | tf_op jit(solution)/shard_map/sweep/pallas_call | solution.py:238
  58.5 0.0 copy-start
  58.5 0.6 %copy-done = f32[4,2]{1,0:T(4,128)S(1)} copy-done((f32[4,2]{1,0:T(4,128)S(1)}, f32[4,2]{1,0:T(4,128)}, u32[]{:S(2)}) %copy-start) | copy-done | bytes 56
  59.2 0.6 %copy.6 = f32[4,2]{0,1:T(2,128)} copy(f32[4,2]{1,0:T(4,128)S(1)} %copy-done) | data formatting | bytes 64 | tf_op jit(solution)/shard_map/sweep/pallas_call | solution.py:238
  59.8 2.6 %copy.8 = bf16[2,256,4,256]{3,2,1,0:T(4,128)(2,1)} copy(bf16[2,256,4,256]{3,2,1,0:T(4,128)(2,1)} %get-tuple-element.6) | data formatting | bytes 2097152
Async XLA Ops:
  58.5 0.7 %copy-start = (f32[4,2]{1,0:T(4,128)S(1)}, f32[4,2]{1,0:T(4,128)}, u32[]{:S(2)}) copy-start(f32[4,2]{1,0:T(4,128)} %get-tuple-element.3) | copy-start | bytes 100

commit v2 on v1

--- a/solution.py
+++ b/solution.py
@@ -9,19 +9,25 @@
 LAYERS = 4
 HALF = 128
 GROUP = 16
+UNROLL = 4
 
 
 def mm(a, b):
     return jnp.dot(a, b, preferred_element_type=jnp.float32)
 
 
-def sweep_kernel(n, chi, d, entries, x_ref, gate_ref, rp_ref, lp_ref, out_ref, rec_ref,
-                 w_ref, site_a, site_b, ahead, back, r_in, a_in, gated, lp_perm, acc, mine, seen,
-                 fs, fr, bs, br, ss, sr):
+def sweep_kernel(n, chi, d, entries, x_hbm, gate_ref, rp_hbm, lp_hbm, out_ref, rec_ref,
+                 x_ref, rp_ref, lp_ref, w_ref, site_a, site_b, ahead, back, r_in, a_in, gated, lp_perm, acc, mine, seen,
+                 xs, ps, fs, fr, bs, br, ss, sr):
     me = lax.axis_index("blk")
     right, left = lax.rem(me + 1, n), lax.rem(me + n - 1, n)
     quarter = chi // d
     barrier = pltpu.get_barrier_semaphore()
+    x_copies = [pltpu.make_async_copy(x_hbm.at[i], x_ref.at[i], xs.at[i]) for i in range(2)]
+    rp_copies = [pltpu.make_async_copy(rp_hbm.at[i], rp_ref.at[i], ps.at[0, i]) for i in range(2)]
+    lp_copies = [pltpu.make_async_copy(lp_hbm.at[i], lp_ref.at[i], ps.at[1, i]) for i in range(2)]
+    for copy in x_copies + [rp_copies[0], lp_copies[0], lp_copies[1], rp_copies[1]]:
+        copy.start()
 
     def greet(k, carry):
         pl.semaphore_signal(barrier, inc=1, device_id={"blk": lax.rem(me + k, n)},
@@ -60,17 +66,20 @@
             w_ref[parity, position * chi:(position + 1) * chi, :] = full.astype(jnp.bfloat16)
 
     mixer(0)
-    mixer(1)
 
     for which, site in ((0, site_a), (1, site_b)):
+        x_copies[which].wait()
+
         def load(k, carry, which=which, site=site):
             block = mm(to_block, x_ref[which, pl.ds(k * quarter, quarter)].reshape(chi, chi)).astype(jnp.bfloat16)
             for p in range(d):
                 for h in range(2):
                     site[h, pl.ds(p * chi + k * quarter, quarter), :] = block[p * quarter:(p + 1) * quarter, h * HALF:(h + 1) * HALF]
             return carry
-        lax.fori_loop(0, d, load, 0)
-    for parity in range(2):
+        lax.fori_loop(0, d, load, 0, unroll=UNROLL)
+
+    def reorder(parity):
+        lp_copies[parity].wait()
         for k in range(2):
             part = mm(lp_ref[parity, :, k * wide:(k + 1) * wide], spread).astype(jnp.bfloat16)
             for s in range(d):
@@ -98,7 +107,7 @@
                             gated[h, pl.ds(s * chi + at * quarter + (2 * pair + j) * GROUP, GROUP), t * HALF:(t + 1) * HALF] = (
                                 mixed[top:top + GROUP, j * HALF:(j + 1) * HALF])
             return carry
-        lax.fori_loop(0, d, tile, 0)
+        lax.fori_loop(0, d, tile, 0, unroll=UNROLL)
 
     def note(value):
         folded = value.reshape(value.shape[0] // 8, 8, value.shape[1])
@@ -131,7 +140,7 @@
             for h in range(2):
                 dst[h, here, :] = value[:, h * HALF:(h + 1) * HALF]
             return carry
-        lax.fori_loop(0, d, tile, 0)
+        lax.fori_loop(0, d, tile, 0, unroll=UNROLL)
 
     def forward(k, h):
         return pltpu.make_async_remote_copy(
@@ -187,11 +196,15 @@
             if layer > 0:
                 power, root = learn(layer - 1)
                 scale = 1.0 / power
+            if layer == 0:
+                rp_copies[0].wait()
             new_left(parity, ahead.at[k], scale)
             if layer == 0:
                 pl.semaphore_wait(barrier, n - 1)
             for h in range(2):
                 forward(k, h).start()
+            if layer == 0:
+                reorder(0)
             for h in range(2):
                 new_right(h, parity, site_b, scale)
         else:
@@ -205,6 +218,10 @@
                 backward(k, h).start()
             new_left(parity, site_b, scale)
         share(layer)
+        if layer == 0:
+            mixer(1)
+            reorder(1)
+            rp_copies[1].wait()
 
     last = LAYERS // 2 - 1
     for h in range(2):
@@ -218,7 +235,7 @@
                 for p in range(d)], axis=0)
             out_ref[which, pl.ds(kk * quarter, quarter)] = (mm(to_plain, block) * shrink).astype(jnp.bfloat16).reshape(quarter, d, chi)
             return carry
-        lax.fori_loop(0, d, store, 0)
+        lax.fori_loop(0, d, store, 0, unroll=UNROLL)
     for k in range(LAYERS // 2):
         for h in range(2):
             forward(k, h).wait_send()
@@ -232,6 +249,7 @@
     n = lax.axis_size("blk")
     entries = float(n * slots * chi * d * chi)
     vmem = pl.BlockSpec(memory_space=pltpu.VMEM)
+    hbm = pl.BlockSpec(memory_space=pl.ANY)
     half = (2, d * chi, HALF)
     dma = pltpu.SemaphoreType.DMA
     pairs = LAYERS // 2
@@ -239,9 +257,12 @@
         functools.partial(sweep_kernel, n, chi, d, entries),
         out_shape=(jax.ShapeDtypeStruct(tensors.shape, jnp.bfloat16),
                    jax.ShapeDtypeStruct((LAYERS, 2), jnp.float32)),
-        in_specs=[vmem] * 4,
+        in_specs=[hbm, vmem, hbm, hbm],
         out_specs=(vmem, vmem),
         scratch_shapes=[
+            pltpu.VMEM(tensors.shape, jnp.bfloat16),
+            pltpu.VMEM(right_proj.shape, jnp.bfloat16),
+            pltpu.VMEM(left_proj.shape, jnp.bfloat16),
             pltpu.VMEM((2, 2 * d * d * GROUP, d * d * GROUP), jnp.bfloat16),
             pltpu.VMEM(half, jnp.bfloat16),
             pltpu.VMEM(half, jnp.bfloat16),
@@ -254,7 +275,7 @@
             pltpu.VMEM((2, 8, HALF), jnp.float32),
             pltpu.VMEM((LAYERS, 2, HALF), jnp.float32),
             pltpu.VMEM((LAYERS, n - 1, 2, HALF), jnp.float32),
-            dma((pairs, 2)), dma((pairs, 2)), dma((pairs, 2)), dma((pairs, 2)),
+            dma((2,)), dma((2, 2)), dma((pairs, 2)), dma((pairs, 2)), dma((pairs, 2)), dma((pairs, 2)),
             dma((LAYERS,)), dma((LAYERS,)),
         ],
         compiler_params=pltpu.CompilerParams(collective_id=0, has_side_effects=True,

time: 62.6 us -> 55.8 us (0.89)
  Pallas kernels: 57.9 us -> 50.9 us
    pallas_call x1, Pallas kernels: 57.9 us -> 50.9 us  [local(): pl.pallas_call(functools.partial(sweep_kernel, n, chi, d, entries), out_s...]
where the time goes in v2:
time: 55.8 us; the launch traced here: 55.4 us
  Pallas kernels  50.9 us (91%)
  local copies, waits for them, and re-layouts  3.85 us (7%)
  between operations  0.65 us (1%)
    pallas_call x1, Pallas kernels, local(): pl.pallas_call(functools.partial(sweep_kernel, n, chi, d, entries), out_s...  50.9 us
    unnamed x3, local copies, waits for them, and re-layouts  3.2 us

profile of v2, /device:TPU:3, one launch (start us, length us, event | category | flops | bytes accessed | tf_op | source)
XLA Modules:
  0.0 55.4 jit_solution(18323698924703617491)
XLA Ops:
  0.6 50.9 %sweep.1 = (bf16[2,256,4,256]{3,2,1,0:T(4,128)(2,1)}, f32[4,2]{1,0:T(4,128)}) custom-call(bf16[2,256,4,256]{3,2,1,0:T(4,128)(2,1)} %x_hbm.1, f32[2,16,16]{2,1,0:T(8,128)} %gate_ref.1, bf16[2,1024,256]{2,1,0:T(8,128)(2,1)} %rp_hbm.1, bf16[2,256,1024]{2,1,0:T(8,128)(2,1)} %lp_hbm.1), custom_call_target="tpu_custom_call" | custom-call | tf_op jit(solution)/shard_map/sweep/pallas_call | solution.py:256
  51.5 0.0 copy-start
  51.5 0.6 %copy-done = f32[4,2]{1,0:T(4,128)S(1)} copy-done((f32[4,2]{1,0:T(4,128)S(1)}, f32[4,2]{1,0:T(4,128)}, u32[]{:S(2)}) %copy-start) | copy-done | bytes 56
  52.2 0.6 %copy.6 = f32[4,2]{0,1:T(2,128)} copy(f32[4,2]{1,0:T(4,128)S(1)} %copy-done) | data formatting | bytes 64 | tf_op jit(solution)/shard_map/sweep/pallas_call | solution.py:256
  52.8 2.6 %copy.8 = bf16[2,256,4,256]{3,2,1,0:T(4,128)(2,1)} copy(bf16[2,256,4,256]{3,2,1,0:T(4,128)(2,1)} %get-tuple-element.6) | data formatting | bytes 2097152
Async XLA Ops:
  51.5 0.7 %copy-start = (f32[4,2]{1,0:T(4,128)S(1)}, f32[4,2]{1,0:T(4,128)}, u32[]{:S(2)}) copy-start(f32[4,2]{1,0:T(4,128)} %get-tuple-element.3) | copy-start | bytes 100

commit v3 on v2

--- a/solution.py
+++ b/solution.py
@@ -126,7 +126,13 @@
         for t in range(d):
             dst[h, t * chi:(t + 1) * chi, :] = value[:, t * HALF:(t + 1) * HALF]
 
-    def new_left(parity, dst, scale):
+    def piece(k, h, s):
+        here = pl.ds(s * chi, chi)
+        return pltpu.make_async_remote_copy(
+            src_ref=ahead.at[k, h, here], dst_ref=r_in.at[k, h, here], send_sem=fs.at[k, h], recv_sem=fr.at[k, h],
+            device_id={"blk": left}, device_id_type=pl.DeviceIdType.MESH)
+
+    def new_left(parity, dst, scale, early=None):
         def tile(s, carry):
             here = pl.ds(s * chi, chi)
             lhs = jnp.concatenate([gated[0, here, :], gated[1, here, :]], axis=1)
@@ -139,6 +145,8 @@
             value = value.astype(jnp.bfloat16)
             for h in range(2):
                 dst[h, here, :] = value[:, h * HALF:(h + 1) * HALF]
+            if early is not None:
+                piece(early, 0, s).start()
             return carry
         lax.fori_loop(0, d, tile, 0, unroll=UNROLL)
 
@@ -198,10 +206,10 @@
                 scale = 1.0 / power
             if layer == 0:
                 rp_copies[0].wait()
-            new_left(parity, ahead.at[k], scale)
+            new_left(parity, ahead.at[k], scale, k if k > 0 else None)
             if layer == 0:
                 pl.semaphore_wait(barrier, n - 1)
-            for h in range(2):
+            for h in range(1 if k > 0 else 0, 2):
                 forward(k, h).start()
             if layer == 0:
                 reorder(0)

time: 55.8 us -> 55.6 us (level)
  no operation moved by 1% of the time
where the time goes in v3:
time: 55.6 us; the launch traced here: 55.1 us
  Pallas kernels  50.6 us (91%)
  local copies, waits for them, and re-layouts  3.85 us (7%)
  between operations  0.65 us (1%)
    pallas_call x1, Pallas kernels, local(): pl.pallas_call(functools.partial(sweep_kernel, n, chi, d, entries), out_s...  50.6 us
    unnamed x3, local copies, waits for them, and re-layouts  3.2 us

profile of v3, /device:TPU:3, one launch (start us, length us, event | category | flops | bytes accessed | tf_op | source)
XLA Modules:
  0.0 55.1 jit_solution(13842737327499746019)
XLA Ops:
  0.6 50.6 %sweep.1 = (bf16[2,256,4,256]{3,2,1,0:T(4,128)(2,1)}, f32[4,2]{1,0:T(4,128)}) custom-call(bf16[2,256,4,256]{3,2,1,0:T(4,128)(2,1)} %x_hbm.1, f32[2,16,16]{2,1,0:T(8,128)} %gate_ref.1, bf16[2,1024,256]{2,1,0:T(8,128)(2,1)} %rp_hbm.1, bf16[2,256,1024]{2,1,0:T(8,128)(2,1)} %lp_hbm.1), custom_call_target="tpu_custom_call" | custom-call | tf_op jit(solution)/shard_map/sweep/pallas_call | solution.py:264
  51.2 0.0 copy-start
  51.2 0.6 %copy-done = f32[4,2]{1,0:T(4,128)S(1)} copy-done((f32[4,2]{1,0:T(4,128)S(1)}, f32[4,2]{1,0:T(4,128)}, u32[]{:S(2)}) %copy-start) | copy-done | bytes 56
  51.9 0.6 %copy.6 = f32[4,2]{0,1:T(2,128)} copy(f32[4,2]{1,0:T(4,128)S(1)} %copy-done) | data formatting | bytes 64 | tf_op jit(solution)/shard_map/sweep/pallas_call | solution.py:264
  52.5 2.6 %copy.8 = bf16[2,256,4,256]{3,2,1,0:T(4,128)(2,1)} copy(bf16[2,256,4,256]{3,2,1,0:T(4,128)(2,1)} %get-tuple-element.6) | data formatting | bytes 2097152
Async XLA Ops:
  51.2 0.7 %copy-start = (f32[4,2]{1,0:T(4,128)S(1)}, f32[4,2]{1,0:T(4,128)}, u32[]{:S(2)}) copy-start(f32[4,2]{1,0:T(4,128)} %get-tuple-element.3) | copy-start | bytes 100
